TPU v7x, 512 devices: a whole 4x8x8 slice. The times are simulated.
512 devices in a mesh: row: 16 (over x, z_lo), col: 32 (over y, z_hi, core).
Axes of the slice: x: 4, y: 8, z: 8 (z_hi: 2, z_lo: 4; z = z_hi * 4 + z_lo), core: 2. Of those that a mesh axis runs over, the one named last changes fastest.
Arguments:
- covariance: float32 [16384, 16384], P('row', 'col'), may hold values from -7 to 14, as said below
- wind_mask: int32 [2, 16384], replicated, may hold values 0 or 1
- wind_speed: float32 [2, 16384], replicated, may hold values from 0.02 to 0.3
- obs_cells: int32 [256, 128], replicated, may hold values from 0 to 16383
- obs_scale: float32 [256], replicated, may hold values from 0.05 to 0.2
- gain: bfloat16 [16384, 256], P('row'), may hold values from -0.375 to 0.375
Outputs:
- updated: float32 [16384, 16384], P('row', 'col')
Inputs may be any that keep to these rules, and one draw needn't show every extreme that they name: A covariance window.
All inputs are finite; a program needn't handle non-finite values.
Results may differ from a plain program's by a relative error of at most 0.0003.
Values sent between devices are 32-bit elements; how exact they have to be, the bound alone decides.
No kernel may reach another device: no remote copies, remote signals or barrier semaphores. Data moves between devices by JAX's collectives and lax.ppermute only.
A program may use at most 64 MiB of HBM per device.

v0:
```python
import jax
import jax.numpy as jnp
from jax import lax
from jax.sharding import PartitionSpec as P

MAPX = 256
diffusion = 0.05


def extended_2(cells, sides, width):
    for axis, dim in sides:
        count = lax.axis_size(axis)
        ends = count - 1
        head = lax.slice_in_dim(cells, 0, width, axis=dim)
        tail = lax.slice_in_dim(cells, cells.shape[dim] - width, cells.shape[dim], axis=dim)
        cells = jnp.concatenate(
            [
                lax.ppermute(tail, axis, [(i, (i + 1) % count) for i in range(ends)]),
                cells,
                lax.ppermute(head, axis, [((i + 1) % count, i) for i in range(ends)]),
            ],
            axis=dim,
        )
    return cells


def coefficients(wind_mask, wind_speed):
    cell_total = wind_speed.shape[1]
    cells = jnp.arange(cell_total, dtype=jnp.int32)
    map_column = cells % MAPX
    map_row = cells // MAPX
    last_row = cell_total // MAPX - 1
    speed_x = wind_speed[0]
    speed_y = wind_speed[1]
    sign_x = wind_mask[0].astype(jnp.float32)
    sign_y = wind_mask[1].astype(jnp.float32)
    middle = 1.0 - speed_x - speed_y - 4.0 * diffusion
    western = jnp.where(map_column > 0, speed_x * sign_x + diffusion, 0.0)
    eastern = jnp.where(map_column < MAPX - 1, speed_x * (1.0 - sign_x) + diffusion, 0.0)
    northern = jnp.where(map_row > 0, speed_y * sign_y + diffusion, 0.0)
    southern = jnp.where(map_row < last_row, speed_y * (1.0 - sign_y) + diffusion, 0.0)
    return jnp.stack([middle, western, eastern, northern, southern])


def transport(extended, coef, along_dim):
    length = extended.shape[along_dim] - 2 * MAPX
    if along_dim == 0:
        weights = coef[:, :, None]
    else:
        weights = coef[:, None, :]

    def window_at(offset):
        return lax.slice_in_dim(extended, offset, offset + length, axis=along_dim)

    result = weights[0] * window_at(MAPX) + weights[1] * window_at(MAPX - 1)
    result = result + weights[2] * window_at(MAPX + 1)
    result = result + weights[3] * window_at(0) + weights[4] * window_at(2 * MAPX)
    return result


def local(covariance, wind_mask, wind_speed, obs_cells, obs_scale, gain):
    row_count, col_count = covariance.shape
    table = coefficients(wind_mask, wind_speed)
    row_start = lax.axis_index("row") * row_count
    col_start = lax.axis_index("col") * col_count
    row_coef = lax.dynamic_slice_in_dim(table, row_start, row_count, 1)
    col_coef = lax.dynamic_slice_in_dim(table, col_start, col_count, 1)
    moved_field = covariance
    for repeat in range(2):
        extended = extended_2(moved_field, (("row", 0),), MAPX)
        moved_field = transport(extended, row_coef, 0)
        extended = extended_2(moved_field, (("col", 1),), MAPX)
        moved_field = transport(extended, col_coef, 1)
    obs_count, foot_count = obs_cells.shape
    obs_block = 16
    local_cell = (obs_cells - row_start).reshape(obs_count // obs_block, obs_block, foot_count)
    row_ids = jnp.arange(row_count, dtype=jnp.int32)

    def count_block(cell_block):
        hits = (cell_block[:, :, None] == row_ids[None, None, :]).astype(jnp.float32)
        return jnp.sum(hits, axis=1)

    counts = lax.map(count_block, local_cell).reshape(obs_count, row_count)
    select = counts * obs_scale[:, None]
    part_sum = jnp.dot(
        select, moved_field, precision=lax.Precision.HIGHEST, preferred_element_type=jnp.float32
    )
    gain_panel = gain.astype(jnp.float32)
    observed = lax.psum(part_sum, "row")
    update = jnp.dot(
        gain_panel, observed, precision=lax.Precision.HIGHEST, preferred_element_type=jnp.float32
    )
    return moved_field - update


def solution(mesh):
    placed = (P("row", "col"), P(), P(), P(), P(), P("row", None))
    return jax.shard_map(
        local, mesh=mesh, in_specs=placed, out_specs=P("row", "col"), check_vma=False
    )
```

profile of v0, /device:TPU:8, one launch (start us, length us, event | category | flops | bytes accessed | tf_op | source)
XLA Modules:
  0.0 402.4 jit_solution(15827598846107994043)
XLA Ops:
  6.5 2.0 copy.13
  8.6 1.1 fusion.45
  9.6 5.1 %collective-permute-start = (f32[256,512]{0,1:T(8,128)}, f32[256,512]{0,1:T(8,128)}, u32[]{:S(2)}, u32[]{:S(2)}) collective-permute-start(f32[256,512]{0,1:T(8,128)} %get-tuple-element.48), channel_id=1, source_target_pairs={{0,32},{32,64},{64,96},{96,128},{128,160},{160,192},{192,224},{224... | collective-permute-start | bytes 1572872 | tf_op jit(solution)/shard_map/ppermute | solution.py:18
  14.7 1.3 collective-permute-start.1
  16.0 0.4 compare_select_fusion
  16.4 0.5 stack.2
  17.1 8.3 %collective-permute-done = f32[256,512]{0,1:T(8,128)} collective-permute-done((f32[256,512]{0,1:T(8,128)}, f32[256,512]{0,1:T(8,128)}, u32[]{:S(2)}, u32[]{:S(2)}) %collective-permute-start) | collective-permute-done | bytes 524320 | tf_op jit(solution)/shard_map/ppermute | solution.py:18
  25.4 15.6 %collective-permute-done.1 = f32[256,512]{0,1:T(8,128)} collective-permute-done((f32[256,512]{0,1:T(8,128)}, f32[256,512]{0,1:T(8,128)}, u32[]{:S(2)}, u32[]{:S(2)}) %collective-permute-start.1) | collective-permute-done | bytes 524320 | tf_op jit(solution)/shard_map/ppermute | solution.py:20
  41.0 5.5 %fusion.14 = f32[1024,512]{0,1:T(8,128)S(1)} fusion(f32[1024,512]{0,1:T(8,128)} %copy-done.2, f32[256,512]{0,1:T(8,128)} %collective-permute-done.1, f32[256,512]{0,1:T(8,128)} %collective-permute-done, f32[1024]{0:T(1024)S(1)} %bitcast.36, f32[1024]{0:T(1024)S(1)} %bitcast.30, f32[1024]{0:T(1024)S(1)} %bitcast.32, f32[1024]{0:T(1024)S(1)} %bitcast.34, ...), kind=kLoop, calls=%fused_computation.33 | loop fusion | flops 6815744 | bytes 5263360 | tf_op jit(solution)/shard_map/add | solution.py:57
  46.4 1.5 fusion.44
  47.9 1.9 collective-permute-start.2
  49.8 8.9 %collective-permute-start.3 = (f32[1024,256]{0,1:T(8,128)}, f32[1024,256]{0,1:T(8,128)}, u32[]{:S(2)}, u32[]{:S(2)}) collective-permute-start(f32[1024,256]{0,1:T(8,128)} %get-tuple-element.47), channel_id=1, source_target_pairs={{1,0},{2,1},{3,2},{4,3},{5,4},{6,5},{7,6},{8,7},{9,8},{10,9},{11,1... | collective-permute-start | bytes 3145736 | tf_op jit(solution)/shard_map/ppermute | solution.py:20
  58.8 22.3 %collective-permute-done.2 = f32[1024,256]{0,1:T(8,128)} collective-permute-done((f32[1024,256]{0,1:T(8,128)}, f32[1024,256]{0,1:T(8,128)}, u32[]{:S(2)}, u32[]{:S(2)}) %collective-permute-start.2) | collective-permute-done | bytes 1048608 | tf_op jit(solution)/shard_map/ppermute | solution.py:18
  81.1 2.6 collective-permute-done.3
  83.7 3.3 fusion.30
  87.0 1.3 copy-done.3
  88.4 2.6 collective-permute-start.4
  91.0 1.3 collective-permute-start.5
  92.3 12.9 %collective-permute-done.4 = f32[256,512]{0,1:T(8,128)S(1)} collective-permute-done((f32[256,512]{0,1:T(8,128)S(1)}, f32[256,512]{0,1:T(8,128)S(1)}, u32[]{:S(2)}, u32[]{:S(2)}) %collective-permute-start.4) | collective-permute-done | bytes 524320 | tf_op jit(solution)/shard_map/ppermute | solution.py:18
  105.2 10.1 %collective-permute-done.5 = f32[256,512]{0,1:T(8,128)} collective-permute-done((f32[256,512]{0,1:T(8,128)S(1)}, f32[256,512]{0,1:T(8,128)}, u32[]{:S(2)}, u32[]{:S(2)}) %collective-permute-start.5) | collective-permute-done | bytes 524320 | tf_op jit(solution)/shard_map/ppermute | solution.py:20
  115.3 5.2 %fusion.6 = f32[1024,512]{0,1:T(8,128)S(1)} fusion(f32[1024,512]{0,1:T(8,128)} %copy-done.3, f32[256,512]{0,1:T(8,128)} %collective-permute-done.5, f32[256,512]{0,1:T(8,128)S(1)} %collective-permute-done.4, f32[1024]{0:T(1024)S(1)} %bitcast.37, f32[1024]{0:T(1024)S(1)} %bitcast.31, f32[1024]{0:T(1024)S(1)} %bitcast.33, f32[1024]{0:T(1024)S(1)} %bitcast.35, ...), kind=kLoop, calls=%fused_computation.25 | loop fusion | flops 6815744 | bytes 5263360 | tf_op jit(solution)/shard_map/add | solution.py:57
  120.5 1.5 fusion.42
  121.9 17.8 %collective-permute-start.6 = (f32[1024,256]{0,1:T(8,128)}, f32[1024,256]{0,1:T(8,128)}, u32[]{:S(2)}, u32[]{:S(2)}) collective-permute-start(f32[1024,256]{0,1:T(8,128)} %get-tuple-element.42), channel_id=1, source_target_pairs={{0,1},{1,2},{2,3},{3,4},{4,5},{5,6},{6,7},{7,8},{8,9},{9,10},{10,1... | collective-permute-start | bytes 3145736 | tf_op jit(solution)/shard_map/ppermute | solution.py:18
  139.7 1.9 collective-permute-start.7
  141.7 32.9 %while.11 = (s32[]{:T(128)}, f32[16,16,1024]{2,1,0:T(8,128)}, s32[16,16,128]{2,1,0:T(8,128)S(1)}, s32[]{:T(128)}) while((s32[]{:T(128)}, f32[16,16,1024]{2,1,0:T(8,128)}, s32[16,16,128]{2,1,0:T(8,128)S(1)}, s32[]{:T(128)}) %tuple.42), condition=%wide.region_2.3_spmd.clone, body=%wide.region_0.2_spmd.clone.sunk | while | flops 6275074 | bytes 221753 | solution.py:83
  141.7 1.4 convert_reduce_fusion.2
  143.1 0.6 bitcast_dynamic-update-slice_fusion.2
  143.8 1.4 convert_reduce_fusion.2
  145.2 0.6 bitcast_dynamic-update-slice_fusion.2
  145.8 1.4 convert_reduce_fusion.2
  147.2 0.6 bitcast_dynamic-update-slice_fusion.2
  147.9 1.4 convert_reduce_fusion.2
  149.3 0.6 bitcast_dynamic-update-slice_fusion.2
  149.9 1.4 convert_reduce_fusion.2
  151.3 0.6 bitcast_dynamic-update-slice_fusion.2
  152.0 1.4 convert_reduce_fusion.2
  153.4 0.6 bitcast_dynamic-update-slice_fusion.2
  154.0 1.4 convert_reduce_fusion.2
  155.4 0.6 bitcast_dynamic-update-slice_fusion.2
  156.1 1.4 convert_reduce_fusion.2
  157.5 0.6 bitcast_dynamic-update-slice_fusion.2
  158.1 1.4 convert_reduce_fusion.2
  159.5 0.6 bitcast_dynamic-update-slice_fusion.2
  160.2 1.4 convert_reduce_fusion.2
  161.6 0.6 bitcast_dynamic-update-slice_fusion.2
  162.2 1.4 convert_reduce_fusion.2
  163.6 0.6 bitcast_dynamic-update-slice_fusion.2
  164.3 1.4 convert_reduce_fusion.2
  165.7 0.6 bitcast_dynamic-update-slice_fusion.2
  166.3 1.4 convert_reduce_fusion.2
  167.8 0.6 bitcast_dynamic-update-slice_fusion.2
  168.4 1.4 convert_reduce_fusion.2
  169.8 0.6 bitcast_dynamic-update-slice_fusion.2
  170.4 1.4 convert_reduce_fusion.2
  171.9 0.6 bitcast_dynamic-update-slice_fusion.2
  172.5 1.4 convert_reduce_fusion.2
  173.9 0.6 bitcast_dynamic-update-slice_fusion.2
  174.5 1.4 bitcast_multiply_fusion
  175.9 3.3 fusion.22
  179.3 1.3 copy-done.1
  180.6 2.7 fusion.46
  183.3 206.8 %all-reduce.2.cloned.1.call-done = f32[256,512]{1,0:T(8,128)} async-done(((f32[256,512]{1,0:T(8,128)}), f32[256,512]{1,0:T(8,128)}) %all-reduce.2.cloned.1.call-update) | async-done | bytes 524304 | tf_op jit(solution)/shard_map/psum | solution.py:89
  390.1 3.6 bitcast_subtract_fusion
  393.7 1.8 copy.18
  (39 shorter events, 0.4 us)
Async XLA Ops:
  6.5 383.5 %copy-start = (bf16[1024,256]{1,0:T(8,128)(2,1)S(1)}, bf16[1024,256]{1,0:T(8,128)(2,1)}, u32[]{:S(2)}) copy-start(bf16[1024,256]{1,0:T(8,128)(2,1)} %param.13) | copy-start | bytes 1572868
  6.5 383.5 %all-reduce.2.cloned.1.call-start = ((), (), s32[]{:S(2)}) async-start(), calls=%async_computation | async-start | bytes 1048576 | tf_op jit(solution)/shard_map/psum | solution.py:89
  8.5 32.4 %copy-start.2 = (f32[1024,512]{0,1:T(8,128)}, f32[1024,512]{0,1:T(8,128)S(1)}, u32[]{:S(2)}) copy-start(f32[1024,512]{0,1:T(8,128)S(1)} %copy.13) | copy-start | bytes 6291460
  8.5 7.5 %copy-start.5 = (s32[2,16384]{1,0:T(2,128)S(1)}, s32[2,16384]{1,0:T(2,128)}, u32[]{:S(2)}) copy-start(s32[2,16384]{1,0:T(2,128)} %param.9) | copy-start | bytes 393220
  8.5 7.5 %copy-start.6 = (f32[2,16384]{1,0:T(2,128)S(1)}, f32[2,16384]{1,0:T(2,128)}, u32[]{:S(2)}) copy-start(f32[2,16384]{1,0:T(2,128)} %param.10) | copy-start | bytes 393220
  9.6 15.8 %collective-permute-start = (f32[256,512]{0,1:T(8,128)}, f32[256,512]{0,1:T(8,128)}, u32[]{:S(2)}, u32[]{:S(2)}) collective-permute-start(f32[256,512]{0,1:T(8,128)} %get-tuple-element.48), channel_id=1, source_target_pairs={{0,32},{32,64},{64,96},{96,128},{128,160},{160,192},{192,224},{224... | collective-permute-start | bytes 1572872 | tf_op jit(solution)/shard_map/ppermute | solution.py:18
  14.7 26.3 %collective-permute-start.1 = (f32[256,512]{0,1:T(8,128)}, f32[256,512]{0,1:T(8,128)}, u32[]{:S(2)}, u32[]{:S(2)}) collective-permute-start(f32[256,512]{0,1:T(8,128)} %get-tuple-element.49), channel_id=1, source_target_pairs={{32,0},{64,32},{96,64},{128,96},{160,128},{192,160},{224,192},{256... | collective-permute-start | bytes 1572872 | tf_op jit(solution)/shard_map/ppermute | solution.py:20
  47.9 33.2 %collective-permute-start.2 = (f32[1024,256]{0,1:T(8,128)}, f32[1024,256]{0,1:T(8,128)}, u32[]{:S(2)}, u32[]{:S(2)}) collective-permute-start(f32[1024,256]{0,1:T(8,128)} %get-tuple-element.46), channel_id=1, source_target_pairs={{0,1},{1,2},{2,3},{3,4},{4,5},{5,6},{6,7},{7,8},{8,9},{9,10},{10,1... | collective-permute-start | bytes 3145736 | tf_op jit(solution)/shard_map/ppermute | solution.py:18
  49.8 33.9 %collective-permute-start.3 = (f32[1024,256]{0,1:T(8,128)}, f32[1024,256]{0,1:T(8,128)}, u32[]{:S(2)}, u32[]{:S(2)}) collective-permute-start(f32[1024,256]{0,1:T(8,128)} %get-tuple-element.47), channel_id=1, source_target_pairs={{1,0},{2,1},{3,2},{4,3},{5,4},{6,5},{7,6},{8,7},{9,8},{10,9},{11,1... | collective-permute-start | bytes 3145736 | tf_op jit(solution)/shard_map/ppermute | solution.py:20
  87.0 1.3 copy-start.3
  88.3 4.0 copy-start.4
  88.4 16.8 %collective-permute-start.4 = (f32[256,512]{0,1:T(8,128)S(1)}, f32[256,512]{0,1:T(8,128)S(1)}, u32[]{:S(2)}, u32[]{:S(2)}) collective-permute-start(f32[256,512]{0,1:T(8,128)S(1)} %get-tuple-element.44), channel_id=1, source_target_pairs={{0,32},{32,64},{64,96},{96,128},{128,160},{160,192},{192,224},{224... | collective-permute-start | bytes 1572872 | tf_op jit(solution)/shard_map/ppermute | solution.py:18
  91.0 24.3 %collective-permute-start.5 = (f32[256,512]{0,1:T(8,128)S(1)}, f32[256,512]{0,1:T(8,128)}, u32[]{:S(2)}, u32[]{:S(2)}) collective-permute-start(f32[256,512]{0,1:T(8,128)S(1)} %get-tuple-element.45), channel_id=1, source_target_pairs={{32,0},{64,32},{96,64},{128,96},{160,128},{192,160},{224,192},{256... | collective-permute-start | bytes 1572872 | tf_op jit(solution)/shard_map/ppermute | solution.py:20
  120.5 54.1 %copy-start.7 = (f32[256]{0:T(256)S(1)}, f32[256]{0:T(256)}, u32[]{:S(2)}) copy-start(f32[256]{0:T(256)} %param.12) | copy-start | bytes 3076
  121.9 54.0 %collective-permute-start.6 = (f32[1024,256]{0,1:T(8,128)}, f32[1024,256]{0,1:T(8,128)}, u32[]{:S(2)}, u32[]{:S(2)}) collective-permute-start(f32[1024,256]{0,1:T(8,128)} %get-tuple-element.42), channel_id=1, source_target_pairs={{0,1},{1,2},{2,3},{3,4},{4,5},{5,6},{6,7},{7,8},{8,9},{9,10},{10,1... | collective-permute-start | bytes 3145736 | tf_op jit(solution)/shard_map/ppermute | solution.py:18
  139.7 36.2 %collective-permute-start.7 = (f32[1024,256]{0,1:T(8,128)}, f32[1024,256]{0,1:T(8,128)}, u32[]{:S(2)}, u32[]{:S(2)}) collective-permute-start(f32[1024,256]{0,1:T(8,128)} %get-tuple-element.43), channel_id=1, source_target_pairs={{1,0},{2,1},{3,2},{4,3},{5,4},{6,5},{7,6},{8,7},{9,8},{10,9},{11,1... | collective-permute-start | bytes 3145736 | tf_op jit(solution)/shard_map/ppermute | solution.py:20
  179.2 1.3 copy-start.1
Sparse Core Ops, SparseCore 0:
  183.4 206.5 all-reduce.1
where the time goes:
time: 403 us; the launch traced here: 402 us
  waiting for transfers between devices  278 us (69%)
  other arithmetic  41.6 us (10%)
  starting transfers between devices  40.8 us (10%)
  local copies, waits for them, and re-layouts  21.4 us (5%)
  between operations  13.7 us (3%)
  matrix products  6.35 us (2%)
    psum x1, waiting for transfers between devices, local(): observed = lax.psum(part_sum, 'row')  207 us
    ppermute x4, waiting for transfers between devices, extended_2(): lax.ppermute(tail, axis, [(i, (i + 1) % count) for i in range(ends)])  43.4 us
    ppermute x4, waiting for transfers between devices, extended_2(): lax.ppermute(head, axis, [((i + 1) % count, i) for i in range(ends)])  28.3 us
    ppermute x4, starting transfers between devices, extended_2(): lax.ppermute(tail, axis, [(i, (i + 1) % count) for i in range(ends)])  27.4 us
    reduce_sum x16, other arithmetic, count_block(): return jnp.sum(hits, axis=1)  22.6 us
    add x4, other arithmetic, transport(): result + weights[3] * window_at(0) + weights[4] * window_at(2 * MAPX)  17.2 us
    ppermute x4, starting transfers between devices, extended_2(): lax.ppermute(head, axis, [((i + 1) % count, i) for i in range(ends)])  13.4 us
    dynamic_update_slice x16, local copies, waits for them, and re-layouts, local(): counts = lax.map(count_block, local_cell).reshape(obs_count, row_count)  10.1 us
  transfers between devices with their start and end apart: 9, of which 7 were waited for; matrix products, arithmetic and copies ran while one was open for 9% of the time, Pallas kernels for 0%

commit v1 on v0

--- a/solution.py
+++ b/solution.py
@@ -86,7 +86,8 @@
         select, moved_field, precision=lax.Precision.HIGHEST, preferred_element_type=jnp.float32
     )
     gain_panel = gain.astype(jnp.float32)
-    observed = lax.psum(part_sum, "row")
+    shards = lax.all_gather(part_sum, "row", axis=0, tiled=False)
+    observed = shards.sum(axis=0)
     update = jnp.dot(
         gain_panel, observed, precision=lax.Precision.HIGHEST, preferred_element_type=jnp.float32
     )

time: 403 us -> 430 us (1.067)
  the two profiles are of different devices: /device:TPU:8 before, /device:TPU:1 now
where the time goes in v1:
time: 430 us; the launch traced here: 429 us
  waiting for transfers between devices  286 us (67%)
  starting transfers between devices  53.8 us (13%)
  other arithmetic  46.7 us (11%)
  local copies, waits for them, and re-layouts  22.6 us (5%)
  between operations  13.7 us (3%)
  matrix products  5.98 us (1%)
    all_gather x1, waiting for transfers between devices, local(): shards = lax.all_gather(part_sum, 'row', axis=0, tiled=False)  213 us
    ppermute x4, waiting for transfers between devices, extended_2(): lax.ppermute(tail, axis, [(i, (i + 1) % count) for i in range(ends)])  50.6 us
    ppermute x4, starting transfers between devices, extended_2(): lax.ppermute(tail, axis, [(i, (i + 1) % count) for i in range(ends)])  47.2 us
    ppermute x4, waiting for transfers between devices, extended_2(): lax.ppermute(head, axis, [((i + 1) % count, i) for i in range(ends)])  22.9 us
    reduce_sum x16, other arithmetic, count_block(): return jnp.sum(hits, axis=1)  22.6 us
    add x4, other arithmetic, transport(): result + weights[3] * window_at(0) + weights[4] * window_at(2 * MAPX)  17.8 us
    dynamic_update_slice x16, local copies, waits for them, and re-layouts, local(): counts = lax.map(count_block, local_cell).reshape(obs_count, row_count)  10.2 us
  transfers between devices with their start and end apart: 9, of which 6 were waited for; matrix products, arithmetic and copies ran while one was open for 8% of the time, Pallas kernels for 0%

profile of v1, /device:TPU:1, one launch (start us, length us, event | category | flops | bytes accessed | tf_op | source)
XLA Modules:
  0.0 429.1 jit_solution(9767882837820728476)
XLA Ops:
  6.5 2.0 copy.13
  8.6 1.1 fusion.45
  9.6 5.6 %collective-permute-start = (f32[256,512]{0,1:T(8,128)}, f32[256,512]{0,1:T(8,128)}, u32[]{:S(2)}, u32[]{:S(2)}) collective-permute-start(f32[256,512]{0,1:T(8,128)} %get-tuple-element.48), channel_id=1, source_target_pairs={{0,32},{32,64},{64,96},{96,128},{128,160},{160,192},{192,224},{224... | collective-permute-start | bytes 1572872 | tf_op jit(solution)/shard_map/ppermute | solution.py:18
  15.3 1.3 collective-permute-start.1
  16.6 0.4 compare_select_fusion
  17.0 0.5 stack.2
  17.7 5.3 %collective-permute-done = f32[256,512]{0,1:T(8,128)} collective-permute-done((f32[256,512]{0,1:T(8,128)}, f32[256,512]{0,1:T(8,128)}, u32[]{:S(2)}, u32[]{:S(2)}) %collective-permute-start) | collective-permute-done | bytes 524320 | tf_op jit(solution)/shard_map/ppermute | solution.py:18
  23.0 19.0 %collective-permute-done.1 = f32[256,512]{0,1:T(8,128)} collective-permute-done((f32[256,512]{0,1:T(8,128)}, f32[256,512]{0,1:T(8,128)}, u32[]{:S(2)}, u32[]{:S(2)}) %collective-permute-start.1) | collective-permute-done | bytes 524320 | tf_op jit(solution)/shard_map/ppermute | solution.py:20
  42.0 5.8 %fusion.14 = f32[1024,512]{0,1:T(8,128)S(1)} fusion(f32[1024,512]{0,1:T(8,128)} %copy-done.3, f32[256,512]{0,1:T(8,128)} %collective-permute-done.1, f32[256,512]{0,1:T(8,128)} %collective-permute-done, f32[1024]{0:T(1024)S(1)} %bitcast.38, f32[1024]{0:T(1024)S(1)} %bitcast.32, f32[1024]{0:T(1024)S(1)} %bitcast.34, f32[1024]{0:T(1024)S(1)} %bitcast.36, ...), kind=kLoop, calls=%fused_computation.33 | loop fusion | flops 6815744 | bytes 5263360 | tf_op jit(solution)/shard_map/add | solution.py:57
  47.8 1.5 fusion.44
  49.2 9.5 %collective-permute-start.2 = (f32[1024,256]{0,1:T(8,128)}, f32[1024,256]{0,1:T(8,128)}, u32[]{:S(2)}, u32[]{:S(2)}) collective-permute-start(f32[1024,256]{0,1:T(8,128)} %get-tuple-element.46), channel_id=1, source_target_pairs={{0,1},{1,2},{2,3},{3,4},{4,5},{5,6},{6,7},{7,8},{8,9},{9,10},{10,1... | collective-permute-start | bytes 3145736 | tf_op jit(solution)/shard_map/ppermute | solution.py:18
  58.7 1.9 collective-permute-start.3
  60.8 40.6 %collective-permute-done.2 = f32[1024,256]{0,1:T(8,128)} collective-permute-done((f32[1024,256]{0,1:T(8,128)}, f32[1024,256]{0,1:T(8,128)}, u32[]{:S(2)}, u32[]{:S(2)}) %collective-permute-start.2) | collective-permute-done | bytes 1048608 | tf_op jit(solution)/shard_map/ppermute | solution.py:18
  101.3 3.3 fusion.30
  104.6 1.3 copy-done.4
  106.0 22.3 %collective-permute-start.4 = (f32[256,512]{0,1:T(8,128)S(1)}, f32[256,512]{0,1:T(8,128)S(1)}, u32[]{:S(2)}, u32[]{:S(2)}) collective-permute-start(f32[256,512]{0,1:T(8,128)S(1)} %get-tuple-element.44), channel_id=1, source_target_pairs={{0,32},{32,64},{64,96},{96,128},{128,160},{160,192},{192,224},{224... | collective-permute-start | bytes 1572872 | tf_op jit(solution)/shard_map/ppermute | solution.py:18
  128.3 1.3 collective-permute-start.5
  129.6 4.7 %collective-permute-done.4 = f32[256,512]{0,1:T(8,128)S(1)} collective-permute-done((f32[256,512]{0,1:T(8,128)S(1)}, f32[256,512]{0,1:T(8,128)S(1)}, u32[]{:S(2)}, u32[]{:S(2)}) %collective-permute-start.4) | collective-permute-done | bytes 524320 | tf_op jit(solution)/shard_map/ppermute | solution.py:18
  134.4 4.0 collective-permute-done.5
  138.3 5.4 %fusion.6 = f32[1024,512]{0,1:T(8,128)S(1)} fusion(f32[1024,512]{0,1:T(8,128)} %copy-done.4, f32[256,512]{0,1:T(8,128)} %collective-permute-done.5, f32[256,512]{0,1:T(8,128)S(1)} %collective-permute-done.4, f32[1024]{0:T(1024)S(1)} %bitcast.39, f32[1024]{0:T(1024)S(1)} %bitcast.33, f32[1024]{0:T(1024)S(1)} %bitcast.35, f32[1024]{0:T(1024)S(1)} %bitcast.37, ...), kind=kLoop, calls=%fused_computation.25 | loop fusion | flops 6815744 | bytes 5263360 | tf_op jit(solution)/shard_map/add | solution.py:57
  143.7 1.5 fusion.42
  145.2 9.8 %collective-permute-start.6 = (f32[1024,256]{0,1:T(8,128)}, f32[1024,256]{0,1:T(8,128)}, u32[]{:S(2)}, u32[]{:S(2)}) collective-permute-start(f32[1024,256]{0,1:T(8,128)} %get-tuple-element.42), channel_id=1, source_target_pairs={{0,1},{1,2},{2,3},{3,4},{4,5},{5,6},{6,7},{7,8},{8,9},{9,10},{10,1... | collective-permute-start | bytes 3145736 | tf_op jit(solution)/shard_map/ppermute | solution.py:18
  155.0 2.1 collective-permute-start.7
  157.1 33.0 %while.11 = (s32[]{:T(128)}, f32[16,16,1024]{2,1,0:T(8,128)}, s32[16,16,128]{2,1,0:T(8,128)S(1)}, s32[]{:T(128)}) while((s32[]{:T(128)}, f32[16,16,1024]{2,1,0:T(8,128)}, s32[16,16,128]{2,1,0:T(8,128)S(1)}, s32[]{:T(128)}) %tuple.42), condition=%wide.region_2.3_spmd.clone, body=%wide.region_0.2_spmd.clone.sunk | while | flops 6275074 | bytes 221253 | solution.py:83
  157.1 1.4 convert_reduce_fusion.2
  158.6 0.6 bitcast_dynamic-update-slice_fusion.2
  159.2 1.4 convert_reduce_fusion.2
  160.6 0.6 bitcast_dynamic-update-slice_fusion.2
  161.3 1.4 convert_reduce_fusion.2
  162.7 0.6 bitcast_dynamic-update-slice_fusion.2
  163.3 1.4 convert_reduce_fusion.2
  164.7 0.6 bitcast_dynamic-update-slice_fusion.2
  165.4 1.4 convert_reduce_fusion.2
  166.8 0.6 bitcast_dynamic-update-slice_fusion.2
  167.4 1.4 convert_reduce_fusion.2
  168.8 0.6 bitcast_dynamic-update-slice_fusion.2
  169.5 1.4 convert_reduce_fusion.2
  170.9 0.6 bitcast_dynamic-update-slice_fusion.2
  171.5 1.4 convert_reduce_fusion.2
  173.0 0.6 bitcast_dynamic-update-slice_fusion.2
  173.6 1.4 convert_reduce_fusion.2
  175.0 0.6 bitcast_dynamic-update-slice_fusion.2
  175.7 1.4 convert_reduce_fusion.2
  177.1 0.6 bitcast_dynamic-update-slice_fusion.2
  177.7 1.4 convert_reduce_fusion.2
  179.1 0.6 bitcast_dynamic-update-slice_fusion.2
  179.8 1.4 convert_reduce_fusion.2
  181.2 0.6 bitcast_dynamic-update-slice_fusion.2
  181.8 1.4 convert_reduce_fusion.2
  183.3 0.6 bitcast_dynamic-update-slice_fusion.2
  183.9 1.4 convert_reduce_fusion.2
  185.3 0.6 bitcast_dynamic-update-slice_fusion.2
  186.0 1.4 convert_reduce_fusion.2
  187.4 0.6 bitcast_dynamic-update-slice_fusion.2
  188.0 1.4 convert_reduce_fusion.2
  189.4 0.6 bitcast_dynamic-update-slice_fusion.2
  190.1 1.4 bitcast_multiply_fusion
  191.5 3.3 fusion.22
  194.8 1.3 copy-done.1
  196.1 2.8 fusion.46
  198.9 212.7 %all-gather.3.cloned.1.call-done = f32[4096,512]{1,0:T(8,128)} async-done(((f32[256,512]{1,0:T(8,128)}), f32[4096,512]{1,0:T(8,128)}) %all-gather.3.cloned.1.call-update) | async-done | bytes 8388624 | tf_op jit(solution)/shard_map/all_gather | solution.py:89
  411.6 4.5 %reduce_sum.18 = f32[256,512]{1,0:T(8,128)S(1)} reduce(f32[16,256,512]{2,1,0:T(8,128)} %bitcast.28, f32[]{:T(128)} %constant.63.clone.1), dimensions={0}, to_apply=%region_3.4 | reduce | flops 1966080 | bytes 8912900 | tf_op jit(solution)/shard_map/reduce_sum | solution.py:90
  416.2 3.2 bitcast_subtract_fusion
  419.4 2.9 copy.18
  (42 shorter events, 0.4 us)
Async XLA Ops:
  6.5 409.6 %copy-start = (bf16[1024,256]{1,0:T(8,128)(2,1)S(1)}, bf16[1024,256]{1,0:T(8,128)(2,1)}, u32[]{:S(2)}) copy-start(bf16[1024,256]{1,0:T(8,128)(2,1)} %param.13) | copy-start | bytes 1572868
  6.5 405.1 %all-gather.3.cloned.1.call-start = ((), (), s32[]{:S(2)}) async-start(), calls=%async_computation | async-start | bytes 8912896 | tf_op jit(solution)/shard_map/all_gather | solution.py:89
  8.5 33.4 %copy-start.3 = (f32[1024,512]{0,1:T(8,128)}, f32[1024,512]{0,1:T(8,128)S(1)}, u32[]{:S(2)}) copy-start(f32[1024,512]{0,1:T(8,128)S(1)} %copy.13) | copy-start | bytes 6291460
  8.5 8.0 %copy-start.6 = (s32[2,16384]{1,0:T(2,128)S(1)}, s32[2,16384]{1,0:T(2,128)}, u32[]{:S(2)}) copy-start(s32[2,16384]{1,0:T(2,128)} %param.9) | copy-start | bytes 393220
  8.5 8.0 %copy-start.7 = (f32[2,16384]{1,0:T(2,128)S(1)}, f32[2,16384]{1,0:T(2,128)}, u32[]{:S(2)}) copy-start(f32[2,16384]{1,0:T(2,128)} %param.10) | copy-start | bytes 393220
  9.6 13.4 %collective-permute-start = (f32[256,512]{0,1:T(8,128)}, f32[256,512]{0,1:T(8,128)}, u32[]{:S(2)}, u32[]{:S(2)}) collective-permute-start(f32[256,512]{0,1:T(8,128)} %get-tuple-element.48), channel_id=1, source_target_pairs={{0,32},{32,64},{64,96},{96,128},{128,160},{160,192},{192,224},{224... | collective-permute-start | bytes 1572872 | tf_op jit(solution)/shard_map/ppermute | solution.py:18
  15.3 26.7 %collective-permute-start.1 = (f32[256,512]{0,1:T(8,128)}, f32[256,512]{0,1:T(8,128)}, u32[]{:S(2)}, u32[]{:S(2)}) collective-permute-start(f32[256,512]{0,1:T(8,128)} %get-tuple-element.49), channel_id=1, source_target_pairs={{32,0},{64,32},{96,64},{128,96},{160,128},{192,160},{224,192},{256... | collective-permute-start | bytes 1572872 | tf_op jit(solution)/shard_map/ppermute | solution.py:20
  49.2 52.1 %collective-permute-start.2 = (f32[1024,256]{0,1:T(8,128)}, f32[1024,256]{0,1:T(8,128)}, u32[]{:S(2)}, u32[]{:S(2)}) collective-permute-start(f32[1024,256]{0,1:T(8,128)} %get-tuple-element.46), channel_id=1, source_target_pairs={{0,1},{1,2},{2,3},{3,4},{4,5},{5,6},{6,7},{7,8},{8,9},{9,10},{10,1... | collective-permute-start | bytes 3145736 | tf_op jit(solution)/shard_map/ppermute | solution.py:18
  58.7 42.6 %collective-permute-start.3 = (f32[1024,256]{0,1:T(8,128)}, f32[1024,256]{0,1:T(8,128)}, u32[]{:S(2)}, u32[]{:S(2)}) collective-permute-start(f32[1024,256]{0,1:T(8,128)} %get-tuple-element.47), channel_id=1, source_target_pairs={{1,0},{2,1},{3,2},{4,3},{5,4},{6,5},{7,6},{8,7},{9,8},{10,9},{11,1... | collective-permute-start | bytes 3145736 | tf_op jit(solution)/shard_map/ppermute | solution.py:20
  104.6 1.3 copy-start.4
  105.9 23.7 %copy-start.5 = (s32[256,128]{1,0:T(8,128)S(1)}, s32[256,128]{1,0:T(8,128)}, u32[]{:S(2)}) copy-start(s32[256,128]{1,0:T(8,128)} %param.11) | copy-start | bytes 393220
  106.0 28.4 %collective-permute-start.4 = (f32[256,512]{0,1:T(8,128)S(1)}, f32[256,512]{0,1:T(8,128)S(1)}, u32[]{:S(2)}, u32[]{:S(2)}) collective-permute-start(f32[256,512]{0,1:T(8,128)S(1)} %get-tuple-element.44), channel_id=1, source_target_pairs={{0,32},{32,64},{64,96},{96,128},{128,160},{160,192},{192,224},{224... | collective-permute-start | bytes 1572872 | tf_op jit(solution)/shard_map/ppermute | solution.py:18
  128.3 10.0 %collective-permute-start.5 = (f32[256,512]{0,1:T(8,128)S(1)}, f32[256,512]{0,1:T(8,128)}, u32[]{:S(2)}, u32[]{:S(2)}) collective-permute-start(f32[256,512]{0,1:T(8,128)S(1)} %get-tuple-element.45), channel_id=1, source_target_pairs={{32,0},{64,32},{96,64},{128,96},{160,128},{192,160},{224,192},{256... | collective-permute-start | bytes 1572872 | tf_op jit(solution)/shard_map/ppermute | solution.py:20
  143.7 46.4 %copy-start.8 = (f32[256]{0:T(256)S(1)}, f32[256]{0:T(256)}, u32[]{:S(2)}) copy-start(f32[256]{0:T(256)} %param.12) | copy-start | bytes 3076
  145.2 46.2 %collective-permute-start.6 = (f32[1024,256]{0,1:T(8,128)}, f32[1024,256]{0,1:T(8,128)}, u32[]{:S(2)}, u32[]{:S(2)}) collective-permute-start(f32[1024,256]{0,1:T(8,128)} %get-tuple-element.42), channel_id=1, source_target_pairs={{0,1},{1,2},{2,3},{3,4},{4,5},{5,6},{6,7},{7,8},{8,9},{9,10},{10,1... | collective-permute-start | bytes 3145736 | tf_op jit(solution)/shard_map/ppermute | solution.py:18
  155.0 36.5 %collective-permute-start.7 = (f32[1024,256]{0,1:T(8,128)}, f32[1024,256]{0,1:T(8,128)}, u32[]{:S(2)}, u32[]{:S(2)}) collective-permute-start(f32[1024,256]{0,1:T(8,128)} %get-tuple-element.43), channel_id=1, source_target_pairs={{1,0},{2,1},{3,2},{4,3},{5,4},{6,5},{7,6},{8,7},{9,8},{10,9},{11,1... | collective-permute-start | bytes 3145736 | tf_op jit(solution)/shard_map/ppermute | solution.py:20
  194.8 1.3 copy-start.1
  411.6 4.6 %copy-start.2 = (f32[1024,512]{0,1:T(8,128)S(1)}, f32[1024,512]{0,1:T(8,128)}, u32[]{:S(2)}) copy-start(f32[1024,512]{0,1:T(8,128)} %copy-done.1) | copy-start | bytes 6291460
Sparse Core Ops, SparseCore 0:
  199.0 212.5 all-gather.2
